TPU v7x, 512 devices: a whole 4x8x8 slice. The times are simulated.
512 devices in a mesh: section: 4 (over x), seq: 8 (over y), dp: 16 (over z, core).
Axes of the slice: x: 4, y: 8, z: 8, core: 2. Of those that a mesh axis runs over, the one named last changes fastest.
Arguments:
- queries: bfloat16 [16, 1024, 32, 128], P('dp', 'seq', 'section'), may hold values from -18 to 18
- video_keys: bfloat16 [16, 1024, 32, 128], P('dp', 'seq', 'section'), may hold values from -18 to 18
- video_values: bfloat16 [16, 1024, 32, 128], P('dp', 'seq', 'section'), may hold values from -6 to 6
- cross_queries: bfloat16 [16, 1024, 32, 128], P('dp', 'seq', 'section'), may hold values from -8 to 8
- self_cotangent: bfloat16 [16, 1024, 32, 128], P('dp', 'seq', 'section'), may hold values from -6 to 6
- cross_cotangent: bfloat16 [16, 1024, 32, 128], P('dp', 'seq', 'section'), may hold values from -6 to 6
- caption_states: bfloat16 [16, 512, 4096], P('dp', 'seq'), may hold values from -400 to 400
- caption_gain: float32 [4096], replicated, may hold values from 0.25 to 1.75
- key_weight: bfloat16 [4096, 4096], P('dp', ('section', 'seq')), may hold values from -0.09375 to 0.09375
- value_weight: bfloat16 [4096, 4096], P('dp', ('section', 'seq')), may hold values from -0.09375 to 0.09375
- video_length: int32 [16], replicated, may hold values from 512 to 1024, as said below
- caption_length: int32 [16], replicated, may hold values from 128 to 512, as said below
Outputs:
- query_gradient: bfloat16 [16, 1024, 32, 128], P('dp', 'seq', 'section')
- key_gradient: bfloat16 [16, 1024, 32, 128], P('dp', 'seq', 'section')
- value_gradient: bfloat16 [16, 1024, 32, 128], P('dp', 'seq', 'section')
- cross_query_gradient: bfloat16 [16, 1024, 32, 128], P('dp', 'seq', 'section')
- key_weight_gradient: float32 [4096, 4096], P('dp', ('section', 'seq'))
- value_weight_gradient: float32 [4096, 4096], P('dp', ('section', 'seq'))
Inputs may be any that keep to these rules, and one draw needn't show every extreme that they name: `video_length`: some clip has all 1024 tokens valid. `caption_length`: some clip has all 512 caption tokens valid.
All inputs are finite; a program needn't handle non-finite values.
Results may differ from a plain program's by a relative error of at most 0.018.
Values may be sent and summed in bfloat16 or wider, within the bound.
A program may use at most 64 MiB of HBM per device.

v0:
```python
import math
import jax
import jax.numpy as jnp
from jax import lax
from jax.sharding import PartitionSpec as P

norm_epsilon = 1e-06


def sent_together(arrays, axis, dim, along):
    ends, at = ([], 0)
    for a in arrays[:-1]:
        at += a.shape[along]
        ends.append(at)
    both = jnp.concatenate(arrays, axis=along)
    return tuple(jnp.split(lax.all_gather(both, axis, axis=dim, tiled=True), ends, axis=along))


def side_by_side(arrays, axis, split_dim, concat_dim, along):
    widths = [a.shape[along] for a in arrays]
    both = jnp.concatenate(arrays, axis=along)
    out = lax.all_to_all(both, axis, split_axis=split_dim, concat_axis=concat_dim, tiled=True)
    return tuple(jnp.split(out, [sum(widths[:k]) for k in range(1, len(widths))], axis=along))


def normalize_rows(states, caption_gain):
    values = states.astype(jnp.float32)
    mean_square = jnp.mean(values * values, axis=-1, keepdims=True)
    return (values * lax.rsqrt(mean_square + norm_epsilon) * caption_gain).astype(jnp.bfloat16)


def block_gradients(query_rows, cotangent_rows, key_rows, value_rows, key_limit, score_scale):
    scores = (
        jnp.einsum("qhd,khd->hqk", query_rows, key_rows, preferred_element_type=jnp.float32)
        * score_scale
    )
    columns = lax.broadcasted_iota(jnp.int32, scores.shape, 2)
    scores = jnp.where(columns < key_limit, scores, -jnp.inf)
    maxima = jnp.max(scores, axis=-1, keepdims=True)
    powers = jnp.exp(scores - maxima)
    weights = powers / jnp.sum(powers, axis=-1, keepdims=True)
    weights_low = weights.astype(jnp.bfloat16)
    weight_grad = jnp.einsum(
        "qhd,khd->hqk", cotangent_rows, value_rows, preferred_element_type=jnp.float32
    )
    row_total = jnp.sum(weights * weight_grad, axis=-1, keepdims=True)
    score_grad = (weights * (weight_grad - row_total) * score_scale).astype(jnp.bfloat16)
    query_grad = jnp.einsum(
        "hqk,khd->qhd", score_grad, key_rows, preferred_element_type=jnp.float32
    )
    key_grad = jnp.einsum(
        "hqk,qhd->khd", score_grad, query_rows, preferred_element_type=jnp.float32
    )
    value_grad = jnp.einsum(
        "hqk,qhd->khd", weights_low, cotangent_rows, preferred_element_type=jnp.float32
    )
    return (query_grad, key_grad, value_grad)


def attention_gradients(query_set, cotangent_set, key_set, value_set, key_limit, score_scale):
    row_count = query_set.shape[0]
    block_rows = math.gcd(row_count, 512)
    block_count = row_count // block_rows
    query_blocks = query_set.reshape((block_count, block_rows) + query_set.shape[1:])
    cotangent_blocks = cotangent_set.reshape((block_count, block_rows) + cotangent_set.shape[1:])

    def advance(totals, inputs):
        query_grad, key_grad, value_grad = block_gradients(
            inputs[0], inputs[1], key_set, value_set, key_limit, score_scale
        )
        return ((totals[0] + key_grad, totals[1] + value_grad), query_grad)

    empty = jnp.zeros(key_set.shape, jnp.float32)
    totals, query_grads = lax.scan(advance, (empty, empty), (query_blocks, cotangent_blocks))
    return (query_grads.reshape(query_set.shape), totals[0], totals[1])


def local(
    queries,
    video_keys,
    video_values,
    cross_queries,
    self_cotangent,
    cross_cotangent,
    caption_states,
    caption_gain,
    key_weight,
    value_weight,
    video_length,
    caption_length,
):
    head_size = queries.shape[3]
    score_scale = 1.0 / math.sqrt(head_size)
    head_width = key_weight.shape[1]
    local_heads = head_width // head_size
    normed = normalize_rows(lax.all_gather(caption_states, "seq", axis=1, tiled=True), caption_gain)
    normed_text = normed[0]
    caption_rows = normed_text.shape[0]
    pieces = sent_together((key_weight, value_weight), "dp", 0, 1)
    columns = normed_text
    text_keys = jnp.dot(columns, pieces[0], preferred_element_type=jnp.float32)
    text_values = jnp.dot(columns, pieces[1], preferred_element_type=jnp.float32)
    text_keys = text_keys.astype(jnp.bfloat16).reshape(caption_rows, local_heads, head_size)
    text_values = text_values.astype(jnp.bfloat16).reshape(caption_rows, local_heads, head_size)
    gathered = side_by_side(
        (queries, video_keys, video_values, cross_queries, self_cotangent, cross_cotangent),
        "seq",
        2,
        1,
        0,
    )
    head_queries, head_keys, head_values, head_cross, self_rows, cross_rows = (
        tensor[0] for tensor in gathered
    )
    clip_index = lax.axis_index("dp")
    video_limit = lax.dynamic_index_in_dim(video_length, clip_index, 0, keepdims=False)
    caption_limit = lax.dynamic_index_in_dim(caption_length, clip_index, 0, keepdims=False)
    positions = lax.broadcasted_iota(jnp.int32, (head_queries.shape[0], 1, 1), 0)
    nothing = jnp.zeros((), jnp.bfloat16)
    self_rows = jnp.where(positions < video_limit, self_rows, nothing)
    cross_rows = jnp.where(positions < video_limit, cross_rows, nothing)
    query_grad, key_grad, value_grad = attention_gradients(
        head_queries, self_rows, head_keys, head_values, video_limit, score_scale
    )
    cross_grad, text_key_grad, text_value_grad = attention_gradients(
        head_cross, cross_rows, text_keys, text_values, caption_limit, score_scale
    )
    returned = side_by_side(
        (
            query_grad.astype(jnp.bfloat16)[None],
            key_grad.astype(jnp.bfloat16)[None],
            value_grad.astype(jnp.bfloat16)[None],
            cross_grad.astype(jnp.bfloat16)[None],
        ),
        "seq",
        1,
        2,
        0,
    )
    key_cot = text_key_grad.astype(jnp.bfloat16).reshape(caption_rows, head_width)
    value_cot = text_value_grad.astype(jnp.bfloat16).reshape(caption_rows, head_width)
    stacked = jnp.concatenate((key_cot, value_cot), axis=1)
    contract_rows = (((0,), (0,)), ((), ()))
    columns = normed_text
    gradients = lax.psum_scatter(
        lax.dot_general(columns, stacked, contract_rows, preferred_element_type=jnp.float32).astype(
            jnp.bfloat16
        ),
        "dp",
        scatter_dimension=0,
        tiled=True,
    ).astype(jnp.float32)
    return (
        returned[0],
        returned[1],
        returned[2],
        returned[3],
        gradients[:, :head_width],
        gradients[:, head_width:],
    )


def solution(mesh):
    placed = (
        P("dp", "seq", "section", None),
        P("dp", "seq", "section", None),
        P("dp", "seq", "section", None),
        P("dp", "seq", "section", None),
        P("dp", "seq", "section", None),
        P("dp", "seq", "section", None),
        P("dp", "seq", None),
        P(),
        P("dp", ("section", "seq")),
        P("dp", ("section", "seq")),
        P(),
        P(),
    )
    return jax.shard_map(
        local,
        mesh=mesh,
        in_specs=placed,
        out_specs=(
            P("dp", "seq", "section", None),
            P("dp", "seq", "section", None),
            P("dp", "seq", "section", None),
            P("dp", "seq", "section", None),
            P("dp", ("section", "seq")),
            P("dp", ("section", "seq")),
        ),
        check_vma=False,
    )
```

profile of v0, /device:TPU:12, one launch (start us, length us, event | category | flops | bytes accessed | tf_op | source)
XLA Modules:
  0.0 239.1 jit_solution(1283080764883097908)
XLA Ops:
  8.0 1.5 pad_maximum_fusion.1
  9.6 1.7 copy_dynamic-update-slice_fusion.5
  11.3 1.7 copy_dynamic-update-slice_fusion.4
  16.1 7.5 %all-to-all-start = ((bf16[6,128,8,128]{3,1,0,2:T(8,128)(2,1)}), bf16[6,128,8,128]{3,1,0,2:T(8,128)(2,1)S(1)}, u32[]{:S(2)}, u32[]{:S(2)}) async-start(bf16[6,128,8,128]{3,1,0,2:T(8,128)(2,1)} %copy_dynamic-update-slice_fusion), calls=%async_computation | async-start | bytes 3145728 | tf_op jit(solution)/shard_map/all_to_all | solution.py:22
  25.5 50.6 %all-to-all-done = bf16[6,128,8,128]{3,1,0,2:T(8,128)(2,1)S(1)} async-done(((bf16[6,128,8,128]{3,1,0,2:T(8,128)(2,1)}), bf16[6,128,8,128]{3,1,0,2:T(8,128)(2,1)S(1)}, u32[]{:S(2)}, u32[]{:S(2)}) %all-to-all-start) | async-done | bytes 1572896 | tf_op jit(solution)/shard_map/all_to_all | solution.py:22
  77.1 0.9 select_bitcast_fusion.1
  78.0 21.0 %all-gather.3.cloned.1.call-done = bf16[1,512,4096]{2,1,0:T(8,128)(2,1)} async-done(((bf16[1,64,4096]{2,1,0:T(8,128)(2,1)}), bf16[1,512,4096]{2,1,0:T(8,128)(2,1)}) %all-gather.3.cloned.1.call-update) | async-done | bytes 4194320 | tf_op jit(solution)/shard_map/all_gather | solution.py:96
  99.0 3.1 %fusion.49 = f32[512]{0:T(512)S(1)} fusion(bf16[1,512,4096]{2,1,0:T(8,128)(2,1)} %all-gather.3.cloned.1.call-done), kind=kLoop, calls=%fused_computation.65 | loop fusion | flops 6290944 | bytes 4196352 | tf_op jit(solution)/shard_map/reduce_sum | solution.py:28
  102.1 45.8 %all-gather.5.cloned.1.call-done = bf16[4096,256]{1,0:T(8,128)(2,1)} async-done(((bf16[256,256]{1,0:T(8,128)(2,1)}), bf16[4096,256]{1,0:T(8,128)(2,1)}) %all-gather.5.cloned.1.call-update) | async-done | bytes 2097168 | tf_op jit(solution)/shard_map/all_gather | solution.py:16
  147.9 3.9 %fusion.53 = bf16[512,1,128]{2,0,1:T(8,128)(2,1)S(1)} fusion(bf16[4096,256]{1,0:T(8,128)(2,1)} %all-gather.5.cloned.1.call-done, bf16[1,512,4096]{2,1,0:T(8,128)(2,1)} %all-gather.3.cloned.1.call-done, f32[4096]{0:T(1024)S(1)} %copy-done.9, f32[512]{0:T(512)S(1)} %add_rsqrt_fusion), kind=kOutput, calls=%fused_computation.73 | convolution fusion | flops 545325056 | bytes 5392384 | tf_op jit(solution)/shard_map/dot_general | solution.py:101
  152.4 1.3 fusion.54
  153.7 8.4 %while.31 = (s32[]{:T(128)}, f32[512,1,128]{0,2,1:T(8,128)}, f32[512,1,128]{0,2,1:T(8,128)S(1)}, bf16[2,512,1,128]{3,1,2,0:T(8,128)(2,1)S(1)}, bf16[2,512,1,128]...) while((s32[]{:T(128)}, f32[512,1,128]{0,2,1:T(8,128)}, ...), condition=%wide.region_10.11_spmd.clone, body=%wide.region_6.10_spmd.clone.sunk | while | flops 340524032 | bytes 11164816 | solution.py:74
  156.1 1.0 fusion.112
  159.8 2.0 fusion.112
  162.2 1.1 convert_bitcast_fusion.2
  163.3 5.2 %convolution_convert_fusion = bf16[4096,256]{1,0:T(8,128)(2,1)} fusion(bf16[512,128]{0,1:T(8,128)(2,1)S(1)} %get-tuple-element.309, bf16[512,128]{0,1:T(8,128)(2,1)S(1)} %get-tuple-element.310, bf16[1,512,4096]{2,1,0:T(8,128)(2,1)} %all-gather.3.cloned.1.call-done, f32[4096]{0:T(1024)S(1)} %copy-done.9, f32[512]{0:T(512)S(1)} %add_rsqrt_fusion), kind=kOutput, calls=%fused_computation.68 | convolution fusion | flops 1083703296 | bytes 6572032 | tf_op jit(solution)/shard_map/dot_general | solution.py:146
  168.6 13.7 %while.30 = (s32[]{:T(128)}, f32[1024,1,128]{0,2,1:T(8,128)S(1)}, f32[1024,1,128]{0,2,1:T(8,128)}, bf16[2,512,1,128]{3,1,2,0:T(8,128)(2,1)S(1)}, bf16[2,512,1,12...) while((s32[]{:T(128)}, f32[1024,1,128]{0,2,1:T(8,128)S(1)}, ...), condition=%wide.region_4.5_spmd.clone, body=%wide.region_0.4_spmd.clone.sunk | while | flops 685243904 | bytes 23622340 | solution.py:74
  170.4 2.6 %fusion.102 = f32[1024,1,128]{0,2,1:T(8,128)} fusion(f32[1024,1,128]{0,2,1:T(8,128)} %get-tuple-element.483, pred[]{:T(512)S(6)} %compare.6, bf16[2,512,1,128]{3,1,2,0:T(8,128)(2,1)} %get-tuple-element.499, s32[]{:T(128)} %get-tuple-element.481, f32[512,1024]{1,0:T(8,128)S(1)} %get-tuple-element.420, f32[512]{0:T(512)S(1)} %fusion.100, ...), kind=kOutput, calls=%fused_computation.10.clone.1 | convolution fusion | flops 137101312 | bytes 3282433 | tf_op jit(solution)/shard_map/while/body/eval_jaxpr/hqk,qhd->khd/dot_general | solution.py:54
  177.1 2.8 %fusion.102 = f32[1024,1,128]{0,2,1:T(8,128)} fusion(f32[1024,1,128]{0,2,1:T(8,128)} %get-tuple-element.483, pred[]{:T(512)S(6)} %compare.6, bf16[2,512,1,128]{3,1,2,0:T(8,128)(2,1)} %get-tuple-element.499, s32[]{:T(128)} %get-tuple-element.481, f32[512,1024]{1,0:T(8,128)S(1)} %get-tuple-element.420, f32[512]{0:T(512)S(1)} %fusion.100, ...), kind=kOutput, calls=%fused_computation.10.clone.1 | convolution fusion | flops 137101312 | bytes 3282433 | tf_op jit(solution)/shard_map/while/body/eval_jaxpr/hqk,qhd->khd/dot_general | solution.py:54
  182.3 1.2 copy.73
  183.7 1.1 pad_maximum_fusion
  185.6 34.7 %all_to_all.30 = bf16[4,1024,1,128]{3,0,2,1:T(4,128)(2,1)S(1)} all-to-all(bf16[4,1024,1,128]{3,0,2,1:T(4,128)(2,1)S(1)} %copy.77), channel_id=1, replica_groups=mesh['section'=4,'seq'=8,'dp'=16] {'seq'}, dimensions={1} | all-to-all | bytes 2097152 | tf_op jit(solution)/shard_map/all_to_all | solution.py:22
  224.0 6.9 %reduce-scatter.2.cloned.1.call-done = bf16[256,256]{1,0:T(8,128)(2,1)} async-done(((bf16[4096,256]{1,0:T(8,128)(2,1)}), bf16[256,256]{1,0:T(8,128)(2,1)}) %reduce-scatter.2.cloned.1.call-update) | async-done | bytes 131088 | tf_op jit(solution)/shard_map/reduce_scatter | solution.py:145
  230.9 1.6 fusion.66
  (86 shorter events, 25.4 us)
Async XLA Ops:
  7.2 5.8 %copy-start.3 = (bf16[1,128,8,128]{3,2,1,0:T(8,128)(2,1)S(1)}, bf16[1,128,8,128]{3,2,1,0:T(8,128)(2,1)}, u32[]{:S(2)}) copy-start(bf16[1,128,8,128]{3,2,1,0:T(8,128)(2,1)} %param.18) | copy-start | bytes 786436
  7.2 6.6 %copy-start.4 = (bf16[1,128,8,128]{3,2,1,0:T(8,128)(2,1)S(1)}, bf16[1,128,8,128]{3,2,1,0:T(8,128)(2,1)}, u32[]{:S(2)}) copy-start(bf16[1,128,8,128]{3,2,1,0:T(8,128)(2,1)} %param.19) | copy-start | bytes 786436
  7.2 7.3 %copy-start.5 = (bf16[1,128,8,128]{3,2,1,0:T(8,128)(2,1)S(1)}, bf16[1,128,8,128]{3,2,1,0:T(8,128)(2,1)}, u32[]{:S(2)}) copy-start(bf16[1,128,8,128]{3,2,1,0:T(8,128)(2,1)} %param.20) | copy-start | bytes 786436
  7.2 8.1 %copy-start.6 = (bf16[1,128,8,128]{3,2,1,0:T(8,128)(2,1)S(1)}, bf16[1,128,8,128]{3,2,1,0:T(8,128)(2,1)}, u32[]{:S(2)}) copy-start(bf16[1,128,8,128]{3,2,1,0:T(8,128)(2,1)} %param.21) | copy-start | bytes 786436
  7.2 91.8 %all-gather.3.cloned.1.call-start = ((), (), s32[]{:S(2)}) async-start(), calls=%async_computation.3 | async-start | bytes 4718592 | tf_op jit(solution)/shard_map/all_gather | solution.py:96
  7.9 140.0 %all-gather.5.cloned.1.call-start = ((), (), s32[]{:S(2)}) async-start(), calls=%async_computation.4 | async-start | bytes 2228224 | tf_op jit(solution)/shard_map/all_gather | solution.py:16
  14.5 9.1 %copy-start.10 = (s32[16]{0:T(128)S(1)}, s32[16]{0:T(128)}, u32[]{:S(2)}) copy-start(s32[16]{0:T(128)} %param.26) | copy-start | bytes 196
  14.5 9.8 %copy-start.11 = (s32[16]{0:T(128)S(1)}, s32[16]{0:T(128)}, u32[]{:S(2)}) copy-start(s32[16]{0:T(128)} %param.27) | copy-start | bytes 196
  16.1 60.0 %all-to-all-start = ((bf16[6,128,8,128]{3,1,0,2:T(8,128)(2,1)}), bf16[6,128,8,128]{3,1,0,2:T(8,128)(2,1)S(1)}, u32[]{:S(2)}, u32[]{:S(2)}) async-start(bf16[6,128,8,128]{3,1,0,2:T(8,128)(2,1)} %copy_dynamic-update-slice_fusion), calls=%async_computation | async-start | bytes 3145728 | tf_op jit(solution)/shard_map/all_to_all | solution.py:22
  23.6 207.3 %reduce-scatter.2.cloned.1.call-start = ((), (), s32[]{:S(2)}) async-start(), calls=%async_computation.5 | async-start | bytes 2228224 | tf_op jit(solution)/shard_map/reduce_scatter | solution.py:145
  78.0 70.0 %copy-start.9 = (f32[4096]{0:T(1024)S(1)}, f32[4096]{0:T(1024)}, u32[]{:S(2)}) copy-start(f32[4096]{0:T(1024)} %param.23) | copy-start | bytes 49156
  147.9 4.0 %copy-start = (bf16[1,512,4096]{2,1,0:T(8,128)(2,1)S(1)}, bf16[1,512,4096]{2,1,0:T(8,128)(2,1)}, u32[]{:S(2)}) copy-start(bf16[1,512,4096]{2,1,0:T(8,128)(2,1)} %all-gather.3.cloned.1.call-done) | copy-start | bytes 12582916
  147.9 4.4 %copy-start.8 = (bf16[4096,256]{1,0:T(8,128)(2,1)S(1)}, bf16[4096,256]{1,0:T(8,128)(2,1)}, u32[]{:S(2)}) copy-start(bf16[4096,256]{1,0:T(8,128)(2,1)} %all-gather.5.cloned.1.call-done) | copy-start | bytes 6291460
  162.2 6.3 %copy-start.1 = (bf16[2,512,1,128]{3,1,2,0:T(8,128)(2,1)}, bf16[2,512,1,128]{3,1,2,0:T(8,128)(2,1)S(1)}, u32[]{:S(2)}) copy-start(bf16[2,512,1,128]{3,1,2,0:T(8,128)(2,1)S(1)} %get-tuple-element.107) | copy-start | bytes 786436
  170.3 2.6 %copy-start.2 = (bf16[1024,1,128]{2,0,1:T(8,128)(2,1)S(1)}, bf16[1024,1,128]{2,0,1:T(8,128)(2,1)}, u32[]{:S(2)}) copy-start(bf16[1024,1,128]{2,0,1:T(8,128)(2,1)} %get-tuple-element.500) | copy-start | bytes 786436 | tf_op jit(solution)/shard_map/while
  170.3 2.6 %copy-start.7 = (bf16[2,512,1,128]{3,1,2,0:T(8,128)(2,1)S(1)}, bf16[2,512,1,128]{3,1,2,0:T(8,128)(2,1)}, u32[]{:S(2)}) copy-start(bf16[2,512,1,128]{3,1,2,0:T(8,128)(2,1)} %get-tuple-element.499) | copy-start | bytes 786436 | tf_op jit(solution)/shard_map/while
  177.1 2.8 %copy-start.2 = (bf16[1024,1,128]{2,0,1:T(8,128)(2,1)S(1)}, bf16[1024,1,128]{2,0,1:T(8,128)(2,1)}, u32[]{:S(2)}) copy-start(bf16[1024,1,128]{2,0,1:T(8,128)(2,1)} %get-tuple-element.500) | copy-start | bytes 786436 | tf_op jit(solution)/shard_map/while
  177.1 2.8 %copy-start.7 = (bf16[2,512,1,128]{3,1,2,0:T(8,128)(2,1)S(1)}, bf16[2,512,1,128]{3,1,2,0:T(8,128)(2,1)}, u32[]{:S(2)}) copy-start(bf16[2,512,1,128]{3,1,2,0:T(8,128)(2,1)} %get-tuple-element.499) | copy-start | bytes 786436 | tf_op jit(solution)/shard_map/while
Sparse Core Ops, SparseCore 0:
  10.1 88.8 all-gather.2
  101.7 46.1 all-gather.4
  168.7 62.2 reduce-scatter.1
where the time goes:
time: 240 us; the launch traced here: 239 us
  waiting for transfers between devices  125 us (52%)
  blocking collectives  34.7 us (14%)
  matrix products  26 us (11%)
  local copies, waits for them, and re-layouts  16.8 us (7%)
  other arithmetic  14.5 us (6%)
  between operations  13.9 us (6%)
  starting transfers between devices  7.62 us (3%)
    all_to_all x1, waiting for transfers between devices, side_by_side(): lax.all_to_all(both, axis, split_axis=split_dim, concat_axis=concat_dim,...  50.6 us
    all_gather x1, waiting for transfers between devices, sent_together(): lax.all_gather(both, axis, axis=dim, tiled=True)  45.8 us
    all_to_all x1, blocking collectives, side_by_side(): lax.all_to_all(both, axis, split_axis=split_dim, concat_axis=concat_dim,...  34.7 us
    all_gather x1, waiting for transfers between devices, local(): lax.all_gather(caption_states, 'seq', axis=1, tiled=True)  21 us
    unnamed x29, local copies, waits for them, and re-layouts  9.77 us
    all_to_all x1, starting transfers between devices, side_by_side(): lax.all_to_all(both, axis, split_axis=split_dim, concat_axis=concat_dim,...  7.55 us
    reduce_scatter x1, waiting for transfers between devices, local(): lax.psum_scatter(lax.dot_general(columns, stacked, contract_rows, preferr...  6.91 us
    dot_general x4, matrix products, block_gradients(): jnp.einsum('hqk,qhd->khd', weights_low, cotangent_rows, preferred_element...  6.08 us
  transfers between devices with their start and end apart: 4, of which 4 were waited for; matrix products, arithmetic and copies ran while one was open for 15% of the time, Pallas kernels for 0%

commit v1 on v0

--- a/solution.py
+++ b/solution.py
@@ -5,6 +5,11 @@
 from jax.sharding import PartitionSpec as P
 
 norm_epsilon = 1e-06
+
+
+def swapped_in(x, name, d):
+    outgoing = jnp.stack([x] * lax.axis_size(name))
+    return jnp.concatenate(lax.all_to_all(outgoing, name, 0, 0), axis=d)
 
 
 def sent_together(arrays, axis, dim, along):
@@ -93,7 +98,7 @@
     score_scale = 1.0 / math.sqrt(head_size)
     head_width = key_weight.shape[1]
     local_heads = head_width // head_size
-    normed = normalize_rows(lax.all_gather(caption_states, "seq", axis=1, tiled=True), caption_gain)
+    normed = normalize_rows(swapped_in(caption_states, "seq", 1), caption_gain)
     normed_text = normed[0]
     caption_rows = normed_text.shape[0]
     pieces = sent_together((key_weight, value_weight), "dp", 0, 1)

time: 240 us -> 262 us (1.092)
  the two profiles are of different devices: /device:TPU:12 before, /device:TPU:10 now
where the time goes in v1:
time: 262 us; the launch traced here: 261 us
  waiting for transfers between devices  101 us (39%)
  blocking collectives  77.5 us (30%)
  matrix products  25 us (10%)
  other arithmetic  18.5 us (7%)
  local copies, waits for them, and re-layouts  17.7 us (7%)
  between operations  14.3 us (5%)
  starting transfers between devices  6.08 us (2%)
    all_to_all x1, waiting for transfers between devices, swapped_in(): return jnp.concatenate(lax.all_to_all(outgoing, name, 0, 0), axis=d)  88.8 us
    all_to_all x2, blocking collectives, side_by_side(): lax.all_to_all(both, axis, split_axis=split_dim, concat_axis=concat_dim,...  77.5 us
    reduce_scatter x1, waiting for transfers between devices, local(): lax.psum_scatter(lax.dot_general(columns, stacked, contract_rows, preferr...  12.4 us
    unnamed x29, local copies, waits for them, and re-layouts  7.71 us
    all_to_all x1, starting transfers between devices, swapped_in(): return jnp.concatenate(lax.all_to_all(outgoing, name, 0, 0), axis=d)  6.04 us
    dot_general x4, matrix products, block_gradients(): jnp.einsum('hqk,qhd->khd', weights_low, cotangent_rows, preferred_element...  6.01 us
    convert_element_type x1, other arithmetic, normalize_rows(): (values * lax.rsqrt(mean_square + norm_epsilon) * caption_gain).astype(jn...  5.81 us
  transfers between devices with their start and end apart: 3, of which 2 were waited for; matrix products, arithmetic and copies ran while one was open for 13% of the time, Pallas kernels for 0%

profile of v1, /device:TPU:10, one launch (start us, length us, event | category | flops | bytes accessed | tf_op | source)
XLA Modules:
  0.0 260.8 jit_solution(1093272946186726352)
XLA Ops:
  7.2 1.0 copy_dynamic-update-slice_fusion.5
  8.2 1.0 copy_dynamic-update-slice_fusion.4
  9.3 1.0 copy_dynamic-update-slice_fusion.3
  10.3 1.0 copy_dynamic-update-slice_fusion.2
  11.5 45.9 %all_to_all.35 = bf16[6,128,8,128]{3,1,0,2:T(8,128)(2,1)S(1)} all-to-all(bf16[6,128,8,128]{3,1,0,2:T(8,128)(2,1)S(1)} %copy_dynamic-update-slice_fusion), channel_id=1, replica_groups=mesh['section'=4,'seq'=8,'dp'=16] {'seq'}, dimensions={2} | all-to-all | bytes 3145728 | tf_op jit(solution)/shard_map/all_to_all | solution.py:27
  57.3 2.5 stack.2
  59.8 6.0 %all-to-all-start.1 = ((bf16[8,1,64,4096]{3,2,1,0:T(8,128)(2,1)}), bf16[8,1,64,4096]{3,2,1,0:T(8,128)(2,1)}, u32[]{:S(2)}, u32[]{:S(2)}) async-start(bf16[8,1,64,4096]{3,2,1,0:T(8,128)(2,1)} %stack.2), calls=%async_computation.1 | async-start | bytes 8388608 | tf_op jit(solution)/shard_map/all_to_all | solution.py:12
  69.6 0.9 select_bitcast_fusion.1
  70.5 88.8 %all-to-all-done.1 = bf16[8,1,64,4096]{3,2,1,0:T(8,128)(2,1)} async-done(((bf16[8,1,64,4096]{3,2,1,0:T(8,128)(2,1)}), bf16[8,1,64,4096]{3,2,1,0:T(8,128)(2,1)}, u32[]{:S(2)}, u32[]{:S(2)}) %all-to-all-start.1) | async-done | bytes 4194336 | tf_op jit(solution)/shard_map/all_to_all | solution.py:12
  159.3 3.1 %multiply_reduce_fusion.2 = f32[8,64]{1,0:T(8,128)S(1)} fusion(bf16[8,1,64,4096]{3,2,1,0:T(8,128)(2,1)} %all-to-all-done.1), kind=kLoop, calls=%fused_computation.66 | loop fusion | flops 6290944 | bytes 4196352 | tf_op jit(solution)/shard_map/reduce_sum | solution.py:33
  162.5 5.8 %fusion.50 = bf16[512,4096]{1,0:T(8,128)(2,1)} fusion(f32[4096]{0:T(1024)S(1)} %copy-done.9, f32[512]{0:T(512)S(1)} %rsqrt.12, bf16[8,1,64,4096]{3,2,1,0:T(8,128)(2,1)} %all-to-all-done.1), kind=kLoop, calls=%fused_computation.65 | loop fusion | flops 8388608 | bytes 8407040 | tf_op jit(solution)/shard_map/convert_element_type | solution.py:34
  168.3 3.9 %fusion.51 = bf16[512,1,128]{2,0,1:T(8,128)(2,1)S(1)} fusion(bf16[512,4096]{1,0:T(8,128)(2,1)} %fusion.50, bf16[4096,256]{1,0:T(8,128)(2,1)} %all-gather.2.cloned.1.call-done), kind=kOutput, calls=%fused_computation.71 | convolution fusion | flops 536936448 | bytes 5373952 | tf_op jit(solution)/shard_map/dot_general | solution.py:106
  172.2 3.1 %fusion.52 = bf16[512,1,128]{2,0,1:T(8,128)(2,1)} fusion(bf16[512,4096]{1,0:T(8,128)(2,1)S(1)} %copy-done, bf16[4096,256]{1,0:T(8,128)(2,1)} %all-gather.2.cloned.1.call-done), kind=kOutput, calls=%fused_computation.72 | convolution fusion | flops 536936448 | bytes 5373952 | tf_op jit(solution)/shard_map/dot_general | solution.py:107
  175.4 7.1 %while.31 = (s32[]{:T(128)}, f32[512,1,128]{0,2,1:T(8,128)S(1)}, f32[512,1,128]{0,2,1:T(8,128)S(1)}, bf16[2,512,1,128]{3,1,2,0:T(8,128)(2,1)S(1)}, bf16[2,512,1,...) while((s32[]{:T(128)}, f32[512,1,128]{0,2,1:T(8,128)S(1)}, ...), condition=%wide.region_10.11_spmd.clone, body=%wide.region_6.10_spmd.clone.sunk | while | flops 340524032 | bytes 11689132 | solution.py:79
  182.6 4.9 %convolution_convert_fusion = bf16[4096,256]{1,0:T(8,128)(2,1)} fusion(bf16[512,4096]{1,0:T(8,128)(2,1)} %fusion.50, bf16[512,128]{0,1:T(8,128)(2,1)S(1)} %get-tuple-element.333, bf16[512,128]{0,1:T(8,128)(2,1)S(1)} %get-tuple-element.334), kind=kOutput, calls=%fused_computation.67 | convolution fusion | flops 1075314688 | bytes 6553600 | tf_op jit(solution)/shard_map/dot_general | solution.py:151
  187.6 13.7 %while.30 = (s32[]{:T(128)}, f32[1024,1,128]{0,2,1:T(8,128)S(1)}, f32[1024,1,128]{0,2,1:T(8,128)}, bf16[2,512,1,128]{3,1,2,0:T(8,128)(2,1)S(1)}, bf16[2,512,1,12...) while((s32[]{:T(128)}, f32[1024,1,128]{0,2,1:T(8,128)S(1)}, ...), condition=%wide.region_4.5_spmd.clone, body=%wide.region_0.4_spmd.clone.sunk | while | flops 685243904 | bytes 23622340 | solution.py:79
  189.4 2.5 fusion.100
  196.1 2.7 %fusion.100 = f32[1024,1,128]{0,2,1:T(8,128)} fusion(f32[1024,1,128]{0,2,1:T(8,128)} %get-tuple-element.507, pred[]{:T(512)S(6)} %compare.6, bf16[2,512,1,128]{3,1,2,0:T(8,128)(2,1)} %get-tuple-element.523, s32[]{:T(128)} %get-tuple-element.505, f32[512,1024]{1,0:T(8,128)S(1)} %get-tuple-element.444, f32[512]{0:T(512)S(1)} %fusion.98, ...), kind=kOutput, calls=%fused_computation.10.clone.1 | convolution fusion | flops 137101312 | bytes 3282433 | tf_op jit(solution)/shard_map/while/body/eval_jaxpr/hqk,qhd->khd/dot_general | solution.py:59
  201.3 1.2 copy.94
  202.7 1.1 pad_maximum_fusion
  204.6 31.7 %all_to_all.36 = bf16[4,1024,1,128]{3,0,2,1:T(4,128)(2,1)S(1)} all-to-all(bf16[4,1024,1,128]{3,0,2,1:T(4,128)(2,1)S(1)} %copy.98), channel_id=1, replica_groups=mesh['section'=4,'seq'=8,'dp'=16] {'seq'}, dimensions={1} | all-to-all | bytes 2097152 | tf_op jit(solution)/shard_map/all_to_all | solution.py:27
  236.5 0.9 copy.100
  240.0 12.4 %reduce-scatter.2.cloned.1.call-done = bf16[256,256]{1,0:T(8,128)(2,1)} async-done(((bf16[4096,256]{1,0:T(8,128)(2,1)}), bf16[256,256]{1,0:T(8,128)(2,1)}) %reduce-scatter.2.cloned.1.call-update) | async-done | bytes 131088 | tf_op jit(solution)/shard_map/reduce_scatter | solution.py:150
  252.4 1.6 fusion.61
  (91 shorter events, 23.0 us)
Async XLA Ops:
  7.2 4.1 %copy-start.4 = (bf16[1,128,8,128]{3,2,1,0:T(8,128)(2,1)S(1)}, bf16[1,128,8,128]{3,2,1,0:T(8,128)(2,1)}, u32[]{:S(2)}) copy-start(bf16[1,128,8,128]{3,2,1,0:T(8,128)(2,1)} %param.20) | copy-start | bytes 786436
  7.2 4.2 %copy-start.5 = (bf16[1,128,8,128]{3,2,1,0:T(8,128)(2,1)S(1)}, bf16[1,128,8,128]{3,2,1,0:T(8,128)(2,1)}, u32[]{:S(2)}) copy-start(bf16[1,128,8,128]{3,2,1,0:T(8,128)(2,1)} %param.21) | copy-start | bytes 786436
  11.3 46.0 %copy-start.2 = (bf16[1,64,4096]{2,1,0:T(8,128)(2,1)S(1)}, bf16[1,64,4096]{2,1,0:T(8,128)(2,1)}, u32[]{:S(2)}) copy-start(bf16[1,64,4096]{2,1,0:T(8,128)(2,1)} %param.22) | copy-start | bytes 1572868
  59.8 6.1 %copy-start.7 = (bf16[256,128]{1,0:T(8,128)(2,1)S(1)}, bf16[256,128]{1,0:T(8,128)(2,1)}, u32[]{:S(2)}) copy-start(bf16[256,128]{1,0:T(8,128)(2,1)} %param.25) | copy-start | bytes 196612
  59.8 6.1 %copy-start.8 = (bf16[256,128]{1,0:T(8,128)(2,1)S(1)}, bf16[256,128]{1,0:T(8,128)(2,1)}, u32[]{:S(2)}) copy-start(bf16[256,128]{1,0:T(8,128)(2,1)} %param.24) | copy-start | bytes 196612
  59.8 6.9 %copy-start.10 = (s32[16]{0:T(128)S(1)}, s32[16]{0:T(128)}, u32[]{:S(2)}) copy-start(s32[16]{0:T(128)} %param.26) | copy-start | bytes 196
  59.8 7.5 %copy-start.11 = (s32[16]{0:T(128)S(1)}, s32[16]{0:T(128)}, u32[]{:S(2)}) copy-start(s32[16]{0:T(128)} %param.27) | copy-start | bytes 196
  59.8 99.5 %all-to-all-start.1 = ((bf16[8,1,64,4096]{3,2,1,0:T(8,128)(2,1)}), bf16[8,1,64,4096]{3,2,1,0:T(8,128)(2,1)}, u32[]{:S(2)}, u32[]{:S(2)}) async-start(bf16[8,1,64,4096]{3,2,1,0:T(8,128)(2,1)} %stack.2), calls=%async_computation.1 | async-start | bytes 8388608 | tf_op jit(solution)/shard_map/all_to_all | solution.py:12
  65.9 102.4 %all-gather.2.cloned.1.call-start = ((), (), s32[]{:S(2)}) async-start(), calls=%async_computation.4 | async-start | bytes 2228224 | tf_op jit(solution)/shard_map/all_gather | solution.py:21
  66.6 185.8 %reduce-scatter.2.cloned.1.call-start = ((), (), s32[]{:S(2)}) async-start(), calls=%async_computation.5 | async-start | bytes 2228224 | tf_op jit(solution)/shard_map/reduce_scatter | solution.py:150
  70.5 92.0 %copy-start.9 = (f32[4096]{0:T(1024)S(1)}, f32[4096]{0:T(1024)}, u32[]{:S(2)}) copy-start(f32[4096]{0:T(1024)} %param.23) | copy-start | bytes 49156
  168.3 3.9 %copy-start = (bf16[512,4096]{1,0:T(8,128)(2,1)S(1)}, bf16[512,4096]{1,0:T(8,128)(2,1)}, u32[]{:S(2)}) copy-start(bf16[512,4096]{1,0:T(8,128)(2,1)} %fusion.50) | copy-start | bytes 12582916
  176.8 0.9 copy-start.12
  180.2 0.9 copy-start.12
  182.5 5.0 %copy-start.1 = (bf16[2,512,1,128]{3,1,2,0:T(8,128)(2,1)}, bf16[2,512,1,128]{3,1,2,0:T(8,128)(2,1)S(1)}, u32[]{:S(2)}) copy-start(bf16[2,512,1,128]{3,1,2,0:T(8,128)(2,1)S(1)} %get-tuple-element.107) | copy-start | bytes 786436
  189.3 2.6 copy-start.3
  189.4 2.5 copy-start.6
  196.1 2.7 %copy-start.3 = (bf16[1024,1,128]{2,0,1:T(8,128)(2,1)S(1)}, bf16[1024,1,128]{2,0,1:T(8,128)(2,1)}, u32[]{:S(2)}) copy-start(bf16[1024,1,128]{2,0,1:T(8,128)(2,1)} %get-tuple-element.524) | copy-start | bytes 786436 | tf_op jit(solution)/shard_map/while
  196.1 2.7 %copy-start.6 = (bf16[2,512,1,128]{3,1,2,0:T(8,128)(2,1)S(1)}, bf16[2,512,1,128]{3,1,2,0:T(8,128)(2,1)}, u32[]{:S(2)}) copy-start(bf16[2,512,1,128]{3,1,2,0:T(8,128)(2,1)} %get-tuple-element.523) | copy-start | bytes 786436 | tf_op jit(solution)/shard_map/while
Sparse Core Ops, SparseCore 0:
  69.4 47.0 all-gather.1
  187.6 64.6 reduce-scatter.1
